TPU v7x, 128 devices: a whole 4x4x4 slice. The times are simulated.
128 devices in a mesh: req: 8 (over y, z_hi), mlp: 16 (over z_lo, x, core).
Axes of the slice: x: 4, y: 4, z: 4 (z_hi: 2, z_lo: 2; z = z_hi * 2 + z_lo), core: 2. Of those that a mesh axis runs over, the one named last changes fastest.
Arguments:
- prompt_tokens: bfloat16 [16, 1024, 2048], P('req', None, 'mlp'), may hold values from -6 to 6
- decode_tokens: bfloat16 [32, 2048], P('req', 'mlp'), may hold values from -6 to 6
- prompt_lengths: int32 [16], P('req'), may hold values from 128 to 1024, as said below
- decode_states: float32 [32, 16, 128, 128], P('req', 'mlp'), may hold values from -6 to 6
- w_fio: float32 [2048, 6144], P('req', 'mlp'), may hold values from -0.125 to 0.125
- forget_bias: float32 [2048], P('mlp'), as said below
- head_gain: float32 [2048], P('mlp'), may hold values from 0.1 to 1.9
- w_out: float32 [2048, 2048], P('mlp', 'req'), may hold values from -0.125 to 0.125
- mlp_gain: float32 [2048], replicated, may hold values from 0.1 to 1.9
- w_gu: float32 [2048, 11264], P('req', 'mlp'), may hold values from -0.125 to 0.125
- w_down: float32 [5632, 2048], P('mlp', 'req'), may hold values from -0.078125 to 0.078125
Outputs:
- prompt_out: bfloat16 [16, 1024, 2048], P('req', None, 'mlp')
- decode_out: bfloat16 [32, 2048], P('req', 'mlp')
- prompt_states: float32 [16, 16, 128, 128], P('req', 'mlp')
- decode_next: float32 [32, 16, 128, 128], P('req', 'mlp')
Inputs may be any that keep to these rules, and one draw needn't show every extreme that they name: `prompt_lengths`: slots at or past a prompt's length are padding; one prompt has length 1024 and another 1024 // 8. `forget_bias`: every entry is at least 3 and at most ln(1024) + 1.7.
All inputs are finite; a program needn't handle non-finite values.
Results may differ from a plain program's by a relative error of at most 0.02.
Values may be sent and summed in bfloat16 or wider, within the bound.
No kernel may reach another device: no remote copies, remote signals or barrier semaphores. Data moves between devices by JAX's collectives and lax.ppermute only.
A program may use at most 128 MiB of HBM per device.

v0:
```python
import jax
import jax.numpy as jnp
from jax import lax
from jax.sharding import PartitionSpec as P

BLOCK = 64
epsilon = 1e-05


def add_columns(operand, weights_piece):
    return jnp.dot(operand, weights_piece, preferred_element_type=jnp.float32)


def project_output(source_rows, weights):
    return jnp.dot(
        source_rows,
        lax.all_gather(weights, "req", axis=1, tiled=True),
        preferred_element_type=jnp.float32,
    )


def block_step(carried, forget_block, value_block, query_block, start_row, lengths):
    steps_here = forget_block.shape[1]
    positions = start_row + jnp.arange(steps_here, dtype=jnp.int32)
    alive_mask = (positions[None, :] < lengths[:, None])[:, :, None, None]
    log_forget = jnp.where(alive_mask, jax.nn.log_sigmoid(forget_block), 0.0)
    key_gate = jnp.where(alive_mask, jax.nn.sigmoid(-forget_block), 0.0)
    cumulated = jnp.cumsum(log_forget, axis=1)
    query_tilde = query_block * jnp.exp(cumulated)
    key_tilde = key_gate * jnp.exp(-cumulated)
    scores = jnp.einsum("pthc,pshc->phts", query_tilde, key_tilde, precision=lax.Precision.HIGHEST)
    triangle = jnp.arange(steps_here)[:, None] >= jnp.arange(steps_here)[None, :]
    scores = jnp.where(triangle, scores, 0.0)
    emitted = jnp.einsum("phts,pshv->pthv", scores, value_block, precision=lax.Precision.HIGHEST)
    emitted = emitted + jnp.einsum(
        "pthc,phcv->pthv", query_tilde, carried, precision=lax.Precision.HIGHEST
    )
    emitted = jnp.where(alive_mask, emitted, 0.0)
    last_log = cumulated[:, -1]
    key_decayed = key_gate * jnp.exp(last_log[:, None] - cumulated)
    carried = jnp.exp(last_log)[..., None] * carried + jnp.einsum(
        "pthc,pthv->phcv", key_decayed, value_block, precision=lax.Precision.HIGHEST
    )
    return (carried, emitted)


def on_device(
    prompt_tokens,
    decode_tokens,
    prompt_lengths,
    decode_states,
    w_fio,
    forget_bias,
    head_gain,
    w_out,
    mlp_gain,
    w_gu,
    w_down,
):
    prompts_here, plen, feature_part = prompt_tokens.shape
    heads_here = decode_states.shape[1]
    head_size = decode_states.shape[2]
    prompt_rows = prompts_here * plen
    local_rows = jnp.concatenate(
        [prompt_tokens.reshape(prompt_rows, feature_part), decode_tokens], axis=0
    )
    row_count = local_rows.shape[0]
    x_full = lax.all_gather(local_rows, "mlp", axis=1, tiled=True)
    model_width = x_full.shape[1]
    mixing = add_columns(
        x_full, lax.all_gather(w_fio.astype(jnp.bfloat16), "req", axis=0, tiled=True)
    )
    mixing = mixing.reshape(row_count, heads_here, 3, head_size)
    bias_table = forget_bias.reshape(heads_here, head_size)
    forget_logit = mixing[:, :, 0] + bias_table
    values = mixing[:, :, 1]
    queries = mixing[:, :, 2]
    prompt_forget = forget_logit[:prompt_rows].reshape(prompts_here, plen, heads_here, head_size)
    prompt_values = values[:prompt_rows].reshape(prompts_here, plen, heads_here, head_size)
    prompt_queries = queries[:prompt_rows].reshape(prompts_here, plen, heads_here, head_size)
    start_state = jnp.zeros((prompts_here, heads_here, head_size, head_size), jnp.float32)
    block_total = plen // BLOCK

    def to_blocks(source_array):
        return source_array.reshape(
            prompts_here, block_total, BLOCK, heads_here, head_size
        ).transpose(1, 0, 2, 3, 4)

    def scan_block(carried, inputs):
        forget_block, value_block, query_block, start_row = inputs
        return block_step(
            carried, forget_block, value_block, query_block, start_row, prompt_lengths
        )

    starts = jnp.arange(block_total, dtype=jnp.int32) * BLOCK
    prompt_states, block_outputs = lax.scan(
        scan_block,
        start_state,
        (to_blocks(prompt_forget), to_blocks(prompt_values), to_blocks(prompt_queries), starts),
    )
    prompt_mixed = block_outputs.transpose(1, 0, 2, 3, 4).reshape(
        prompts_here, plen, heads_here, head_size
    )
    decode_logit = forget_logit[prompt_rows:]
    decode_next = (
        jax.nn.sigmoid(decode_logit)[..., None] * decode_states
        + jax.nn.sigmoid(-decode_logit)[..., None] * values[prompt_rows:][:, :, None, :]
    )
    decode_mixed = jnp.einsum(
        "nhcv,nhc->nhv", decode_next, queries[prompt_rows:], precision=lax.Precision.HIGHEST
    )
    mixed_all = jnp.concatenate(
        [prompt_mixed.reshape(prompt_rows, heads_here, head_size), decode_mixed], axis=0
    )
    mean_square = jnp.mean(mixed_all * mixed_all, axis=-1, keepdims=True)
    head_rows = (
        mixed_all * lax.rsqrt(mean_square + epsilon) * head_gain.reshape(heads_here, head_size)
    ).astype(jnp.bfloat16)
    head_rows = head_rows.reshape(row_count, heads_here * head_size)
    offset = lax.axis_index("mlp") * feature_part
    head_terms = project_output(head_rows, w_out.astype(jnp.bfloat16))
    attention = lax.psum_scatter(
        head_terms.astype(jnp.bfloat16), "mlp", scatter_dimension=1, tiled=True
    ).astype(jnp.float32)
    residual = (local_rows.astype(jnp.float32) + attention).astype(jnp.bfloat16)
    residual_wide = residual.astype(jnp.float32)
    square_sum = lax.psum(jnp.sum(residual_wide * residual_wide, axis=1), "mlp")
    row_scale = lax.rsqrt(square_sum / model_width + epsilon)[:, None]
    gain_part = lax.dynamic_slice_in_dim(mlp_gain, offset, feature_part)
    normed_part = (residual_wide * row_scale * gain_part).astype(jnp.bfloat16)
    normed = lax.all_gather(normed_part, "mlp", axis=1, tiled=True)
    gate_up = add_columns(
        normed, lax.all_gather(w_gu.astype(jnp.bfloat16), "req", axis=0, tiled=True)
    )
    hidden_here = w_gu.shape[1] // 2
    hidden = (jax.nn.silu(gate_up[:, :hidden_here]) * gate_up[:, hidden_here:]).astype(jnp.bfloat16)
    down_terms = jnp.dot(
        hidden,
        lax.all_gather(w_down.astype(jnp.bfloat16), "req", axis=1, tiled=True),
        preferred_element_type=jnp.float32,
    )
    down_share = lax.psum_scatter(
        down_terms.astype(jnp.bfloat16), "mlp", scatter_dimension=1, tiled=True
    ).astype(jnp.float32)
    layer_output = (residual_wide + down_share).astype(jnp.bfloat16)
    prompt_out = layer_output[:prompt_rows].reshape(prompts_here, plen, feature_part)
    decode_out = layer_output[prompt_rows:]
    return (prompt_out, decode_out, prompt_states, decode_next)


def solution(mesh):
    placed = (
        P("req", None, "mlp"),
        P("req", "mlp"),
        P("req"),
        P("req", "mlp", None, None),
        P("req", "mlp"),
        P("mlp"),
        P("mlp"),
        P("mlp", "req"),
        P(),
        P("req", "mlp"),
        P("mlp", "req"),
    )
    return jax.shard_map(
        on_device,
        mesh=mesh,
        in_specs=placed,
        out_specs=(
            P("req", None, "mlp"),
            P("req", "mlp"),
            P("req", "mlp", None, None),
            P("req", "mlp", None, None),
        ),
        check_vma=False,
    )
```

profile of v0, /device:TPU:0, one launch (start us, length us, event | category | flops | bytes accessed | tf_op | source)
XLA Modules:
  0.0 637.0 jit_solution(2306237471951861111)
XLA Ops:
  7.2 1.8 convert_element_type.49
  9.1 1.5 pad_maximum_fusion
  10.7 38.0 %all_gather.20 = bf16[128,2048]{1,0:T(8,128)(2,1)} all-gather(bf16[128,256]{1,0:T(8,128)(2,1)S(1)} %convert_element_type.51), channel_id=1, replica_groups=mesh['req'=8,'mlp'=16] {'req'}, dimensions={1}, use_global_device_ids=true | all-gather | bytes 589824 | tf_op jit(solution)/shard_map/all_gather | solution.py:17
  48.7 17.3 %all-gather.8.cloned.1.call-done = bf16[2048,384]{1,0:T(8,128)(2,1)} async-done(((bf16[256,384]{1,0:T(8,128)(2,1)}), bf16[2048,384]{1,0:T(8,128)(2,1)}) %all-gather.8.cloned.1.call-update) | async-done | bytes 1572880 | tf_op jit(solution)/shard_map/all_gather | solution.py:71
  66.1 61.3 %all-gather.6.cloned.1.call-done = bf16[2052,2048]{1,0:T(8,128)(2,1)} async-done(((bf16[2052,128]{1,0:T(8,128)(2,1)}), bf16[2052,2048]{1,0:T(8,128)(2,1)}) %all-gather.6.cloned.1.call-update) | async-done | bytes 8405008 | tf_op jit(solution)/shard_map/all_gather | solution.py:68
  127.4 7.4 %fusion.59 = f32[2052,384]{0,1:T(8,128)S(1)} fusion(bf16[2052,2048]{1,0:T(8,128)(2,1)} %all-gather.6.cloned.1.call-done, bf16[2048,384]{1,0:T(8,128)(2,1)} %all-gather.8.cloned.1.call-done), kind=kOutput, calls=%fused_computation.84 | convolution fusion | flops 3227516928 | bytes 13129728 | tf_op jit(solution)/shard_map/dot_general | solution.py:11
  134.9 1.6 copy-done.3
  137.3 2.2 copy-done.4
  140.8 2.6 copy.47
  143.3 1.3 copy.48
  144.7 108.7 %while.13 = (s32[]{:T(128)}, f32[2,1,128,128]{3,2,0,1:T(8,128)S(1)}, f32[16,2,64,1,128]{4,2,0,1,3:T(8,128)}, s32[16]{0:T(128)S(1)}, s32[2]{0:T(128)S(1)}, /*inde...) while((s32[]{:T(128)}, ...), condition=%wide.region_2.3_spmd.clone, body=%wide.region_0.2_spmd.clone.sunk | while | flops 77050048 | bytes 1596940 | solution.py:96
  148.4 1.7 fusion.93
  150.1 1.3 fusion.91
  155.2 1.7 fusion.93
  162.0 1.7 fusion.93
  163.7 1.3 fusion.91
  168.8 1.7 fusion.93
  170.5 1.3 fusion.91
  175.6 1.7 fusion.93
  177.3 1.3 fusion.91
  182.4 1.7 fusion.93
  184.1 1.3 fusion.91
  189.2 1.7 fusion.93
  190.9 1.3 fusion.91
  196.0 1.7 fusion.93
  197.7 1.3 fusion.91
  202.8 1.7 fusion.93
  209.6 1.7 fusion.93
  216.4 1.7 fusion.93
  223.2 1.7 fusion.93
  229.9 1.7 fusion.93
  236.7 1.7 fusion.93
  243.5 1.7 fusion.93
  250.3 1.7 fusion.93
  254.0 1.6 fusion.49
  255.7 5.6 convolution_convert_fusion.1
  261.3 11.6 %copy.58 = bf16[2052,2048]{0,1:T(8,128)(2,1)} copy(bf16[2052,2048]{1,0:T(8,128)(2,1)} %convolution_convert_fusion.1) | data formatting | bytes 16809984
  275.6 73.2 %reduce-scatter.7.cloned.1.call-done = bf16[128,2052]{1,0:T(8,128)(2,1)} async-done(((bf16[2048,2052]{1,0:T(8,128)(2,1)}), bf16[128,2052]{1,0:T(8,128)(2,1)}) %reduce-scatter.7.cloned.1.call-update) | async-done | bytes 525328
  348.8 1.3 copy.59
  350.5 54.1 %psum.7 = f32[2052]{0:T(1024)S(1)} all-reduce(f32[2052]{0:T(1024)S(1)} %fusion.43), channel_id=1, replica_groups=mesh['req'=8,'mlp'=16] {'mlp'}, use_global_device_ids=true, to_apply=%region_6.7 | all-reduce | flops 2052 | bytes 16416 | tf_op jit(solution)/shard_map/psum | solution.py:127
  406.9 8.9 %all-gather.12.cloned.1.call-done = bf16[2048,704]{0,1:T(8,128)(2,1)} async-done(((bf16[256,704]{0,1:T(8,128)(2,1)}), bf16[2048,704]{0,1:T(8,128)(2,1)}) %all-gather.12.cloned.1.call-update) | async-done | bytes 2883600 | tf_op jit(solution)/shard_map/all_gather | solution.py:133
  415.8 60.6 %all-gather.10.cloned.1.call-done = bf16[2052,2048]{1,0:T(8,128)(2,1)} async-done(((bf16[2052,128]{1,0:T(8,128)(2,1)}), bf16[2052,2048]{1,0:T(8,128)(2,1)}) %all-gather.10.cloned.1.call-update) | async-done | bytes 8405008 | tf_op jit(solution)/shard_map/all_gather | solution.py:131
  476.4 12.6 %fusion.60 = f32[2052,704]{0,1:T(8,128)} fusion(bf16[2052,2048]{1,0:T(8,128)(2,1)} %all-gather.10.cloned.1.call-done, bf16[2048,704]{0,1:T(8,128)(2,1)} %all-gather.12.cloned.1.call-done), kind=kOutput, calls=%fused_computation.85 | convolution fusion | flops 5917114368 | bytes 17067008 | tf_op jit(solution)/shard_map/dot_general | solution.py:11
  489.0 41.2 %all-gather.14.cloned.1.call-done = bf16[352,2048]{1,0:T(8,128)(2,1)} async-done(((bf16[352,256]{1,0:T(8,128)(2,1)}), bf16[352,2048]{1,0:T(8,128)(2,1)}) %all-gather.14.cloned.1.call-update) | async-done | bytes 1441808 | tf_op jit(solution)/shard_map/all_gather | solution.py:139
  530.1 11.1 %convolution_convert_fusion = bf16[2052,2048]{1,0:T(8,128)(2,1)} fusion(bf16[352,2048]{1,0:T(8,128)(2,1)} %all-gather.14.cloned.1.call-done, f32[2052,704]{0,1:T(8,128)} %fusion.60), kind=kOutput, calls=%fused_computation.48 | convolution fusion | flops 2967093504 | bytes 15625216 | tf_op jit(solution)/shard_map/dot_general | solution.py:137
  541.2 11.5 %copy.60 = bf16[2052,2048]{0,1:T(8,128)(2,1)} copy(bf16[2052,2048]{1,0:T(8,128)(2,1)} %convolution_convert_fusion) | data formatting | bytes 16809984
  552.8 74.4 %reduce-scatter.9.cloned.1.call-done = bf16[128,2052]{1,0:T(8,128)(2,1)} async-done(((bf16[2048,2052]{1,0:T(8,128)(2,1)}), bf16[128,2052]{1,0:T(8,128)(2,1)}) %reduce-scatter.9.cloned.1.call-update) | async-done | bytes 525328
  627.2 1.3 copy.61
  (239 shorter events, 80.5 us)
Async XLA Ops:
  7.2 1.9 copy-start
  7.2 3.5 copy-start.11
  7.2 58.9 %all-gather.8.cloned.1.call-start = ((), (), s32[]{:S(2)}) async-start(), calls=%async_computation.3 | async-start | bytes 1769472 | tf_op jit(solution)/shard_map/all_gather | solution.py:71
  9.0 118.4 %all-gather.6.cloned.1.call-start = ((), (), s32[]{:S(2)}) async-start(), calls=%async_computation.2 | async-start | bytes 8947712 | tf_op jit(solution)/shard_map/all_gather | solution.py:68
  10.6 338.2 %reduce-scatter.7.cloned.1.call-start = ((), (), s32[]{:S(2)}) async-start(), calls=%async_computation.7 | async-start | bytes 9469952
  134.8 1.7 copy-start.3
  136.5 0.7 copy-start.14
  137.2 2.3 copy-start.4
  137.3 3.4 copy-start.1
  143.3 1.3 slice-start
  143.3 1.3 copy-start.15
  144.7 108.8 %copy-start.10 = (f32[4,1,128,128]{3,2,1,0:T(8,128)S(1)}, f32[4,1,128,128]{3,2,1,0:T(8,128)}, u32[]{:S(2)}) copy-start(f32[4,1,128,128]{3,2,1,0:T(8,128)} %param.16) | copy-start | bytes 786436
  253.4 7.9 %copy-start.5 = (f32[2,1,128,128]{3,2,0,1:T(8,128)}, f32[2,1,128,128]{3,2,0,1:T(8,128)S(1)}, u32[]{:S(2)}) copy-start(f32[2,1,128,128]{3,2,0,1:T(8,128)S(1)} %get-tuple-element.114) | copy-start | bytes 393220
  253.4 2.3 copy-start.2
  253.4 2.3 copy-start.6
  253.4 2.3 copy-start.13
  253.6 7.7 %copy-start.7 = (f32[4,1,128,128]{3,2,1,0:T(8,128)}, f32[4,1,128,128]{3,2,1,0:T(8,128)S(1)}, u32[]{:S(2)}) copy-start(f32[4,1,128,128]{3,2,1,0:T(8,128)S(1)} %multiply_add_fusion) | copy-start | bytes 786436
  272.9 1.1 copy-start.8
  272.9 77.2 %copy-start.12 = (bf16[4,128]{1,0:T(4,128)(2,1)S(1)}, bf16[4,128]{1,0:T(4,128)(2,1)}, u32[]{:S(2)}) copy-start(bf16[4,128]{1,0:T(4,128)(2,1)} %param.14) | copy-start | bytes 3076
  272.9 142.9 %all-gather.12.cloned.1.call-start = ((), (), s32[]{:S(2)}) async-start(), calls=%async_computation.5 | async-start | bytes 3244032 | tf_op jit(solution)/shard_map/all_gather | solution.py:133
  274.8 201.6 %all-gather.10.cloned.1.call-start = ((), (), s32[]{:S(2)}) async-start(), calls=%async_computation.4 | async-start | bytes 8947712 | tf_op jit(solution)/shard_map/all_gather | solution.py:131
  350.5 55.4 %copy-start.9 = (f32[352,256]{1,0:T(8,128)S(1)}, f32[352,256]{1,0:T(8,128)}, u32[]{:S(2)}) copy-start(f32[352,256]{1,0:T(8,128)} %param.23) | copy-start | bytes 1081348
  405.9 124.3 %all-gather.14.cloned.1.call-start = ((), (), s32[]{:S(2)}) async-start(), calls=%async_computation.6 | async-start | bytes 1622016 | tf_op jit(solution)/shard_map/all_gather | solution.py:139
  406.7 220.6 %reduce-scatter.9.cloned.1.call-start = ((), (), s32[]{:S(2)}) async-start(), calls=%async_computation.8 | async-start | bytes 9469952
Sparse Core Ops, SparseCore 0:
  10.9 55.1 all-gather.7
  67.7 59.6 all-gather.5
  273.0 75.7 reduce-scatter.6
  351.4 64.3 all-gather.11
  417.3 59.0 all-gather.9
  478.4 51.6 all-gather.13
  552.9 74.2 reduce-scatter.8
where the time goes:
time: 641 us; the launch traced here: 637 us
  waiting for transfers between devices  337 us (53%)
  matrix products  121 us (19%)
  blocking collectives  92.2 us (14%)
  local copies, waits for them, and re-layouts  48.2 us (8%)
  other arithmetic  22.7 us (4%)
  between operations  14.4 us (2%)
    unnamed x9, waiting for transfers between devices  148 us
    all_gather x1, waiting for transfers between devices, on_device(): x_full = lax.all_gather(local_rows, 'mlp', axis=1, tiled=True)  61.3 us
    all_gather x1, waiting for transfers between devices, on_device(): normed = lax.all_gather(normed_part, 'mlp', axis=1, tiled=True)  60.6 us
    psum x1, blocking collectives, on_device(): square_sum = lax.psum(jnp.sum(residual_wide * residual_wide, axis=1), 'mlp')  54.1 us
    all_gather x1, waiting for transfers between devices, on_device(): lax.all_gather(w_down.astype(jnp.bfloat16), 'req', axis=1, tiled=True)  41.2 us
    all_gather x1, blocking collectives, project_output(): lax.all_gather(weights, 'req', axis=1, tiled=True)  38 us
    unnamed x37, local copies, waits for them, and re-layouts  31.3 us
    dot_general x16, matrix products, block_step(): jnp.einsum('pthc,phcv->pthv', query_tilde, carried, precision=lax.Precisi...  27.6 us
  transfers between devices with their start and end apart: 7, of which 7 were waited for; matrix products, arithmetic and copies ran while one was open for 3% of the time, Pallas kernels for 0%

commit v1 on v0

--- a/solution.py
+++ b/solution.py
@@ -124,7 +124,9 @@
     ).astype(jnp.float32)
     residual = (local_rows.astype(jnp.float32) + attention).astype(jnp.bfloat16)
     residual_wide = residual.astype(jnp.float32)
-    square_sum = lax.psum(jnp.sum(residual_wide * residual_wide, axis=1), "mlp")
+    square_sum = jnp.sum(
+        lax.all_gather(jnp.sum(residual_wide * residual_wide, axis=1), "mlp"), axis=0
+    )
     row_scale = lax.rsqrt(square_sum / model_width + epsilon)[:, None]
     gain_part = lax.dynamic_slice_in_dim(mlp_gain, offset, feature_part)
     normed_part = (residual_wide * row_scale * gain_part).astype(jnp.bfloat16)

time: 641 us -> 753 us (1.17)
  waiting for transfers between devices: 337 us -> 500 us
  blocking collectives: 92.2 us -> 38 us
    unnamed x9 -> x11, waiting for transfers between devices: 148 us -> 252 us
    all_gather x1, waiting for transfers between devices: 8.91 us -> 66.4 us  [on_device(): lax.all_gather(w_gu.astype(jnp.bfloat16), 'req', axis=0, tiled=True)]
    psum x1 -> x0, blocking collectives: 54.1 us -> none  [on_device(): square_sum = lax.psum(jnp.sum(residual_wide * residual_wide, axis=1), 'mlp')]
    unnamed x37 -> x44, local copies, waits for them, and re-layouts: 31.3 us -> 32.5 us
  transfers between devices with their start and end apart: 7 -> 8, of which waited for: 7 -> 8; matrix products, arithmetic and copies ran while one was open for 3% -> 3% of each run, Pallas kernels for 0% -> 0%
where the time goes in v1:
time: 753 us; the launch traced here: 749 us
  waiting for transfers between devices  500 us (66%)
  matrix products  121 us (16%)
  local copies, waits for them, and re-layouts  50.4 us (7%)
  blocking collectives  38 us (5%)
  other arithmetic  22.7 us (3%)
  between operations  15.1 us (2%)
    unnamed x11, waiting for transfers between devices  252 us
    all_gather x1, waiting for transfers between devices, on_device(): lax.all_gather(w_gu.astype(jnp.bfloat16), 'req', axis=0, tiled=True)  66.4 us
    all_gather x1, waiting for transfers between devices, on_device(): x_full = lax.all_gather(local_rows, 'mlp', axis=1, tiled=True)  61.3 us
    all_gather x1, waiting for transfers between devices, on_device(): normed = lax.all_gather(normed_part, 'mlp', axis=1, tiled=True)  60.9 us
    all_gather x1, waiting for transfers between devices, on_device(): lax.all_gather(w_down.astype(jnp.bfloat16), 'req', axis=1, tiled=True)  41.6 us
    all_gather x1, blocking collectives, project_output(): lax.all_gather(weights, 'req', axis=1, tiled=True)  38 us
    unnamed x44, local copies, waits for them, and re-layouts  32.5 us
    dot_general x16, matrix products, block_step(): jnp.einsum('pthc,phcv->pthv', query_tilde, carried, precision=lax.Precisi...  27.6 us
  transfers between devices with their start and end apart: 8, of which 8 were waited for; matrix products, arithmetic and copies ran while one was open for 3% of the time, Pallas kernels for 0%

profile of v1, /device:TPU:0, one launch (start us, length us, event | category | flops | bytes accessed | tf_op | source)
XLA Modules:
  0.0 748.5 jit_solution(11671130516654439487)
XLA Ops:
  7.2 1.8 convert_element_type.49
  9.1 1.5 pad_maximum_fusion
  10.7 38.0 %all_gather.26 = bf16[128,2048]{1,0:T(8,128)(2,1)} all-gather(bf16[128,256]{1,0:T(8,128)(2,1)S(1)} %convert_element_type.51), channel_id=1, replica_groups=mesh['req'=8,'mlp'=16] {'req'}, dimensions={1}, use_global_device_ids=true | all-gather | bytes 589824 | tf_op jit(solution)/shard_map/all_gather | solution.py:17
  48.7 17.4 %all-gather.9.cloned.1.call-done = bf16[2048,384]{1,0:T(8,128)(2,1)} async-done(((bf16[256,384]{1,0:T(8,128)(2,1)}), bf16[2048,384]{1,0:T(8,128)(2,1)}) %all-gather.9.cloned.1.call-update) | async-done | bytes 1572880 | tf_op jit(solution)/shard_map/all_gather | solution.py:71
  66.1 61.3 %all-gather.7.cloned.1.call-done = bf16[2052,2048]{1,0:T(8,128)(2,1)} async-done(((bf16[2052,128]{1,0:T(8,128)(2,1)}), bf16[2052,2048]{1,0:T(8,128)(2,1)}) %all-gather.7.cloned.1.call-update) | async-done | bytes 8405008 | tf_op jit(solution)/shard_map/all_gather | solution.py:68
  127.4 7.4 fusion.59
  134.9 1.6 copy-done.3
  137.3 2.2 copy-done.4
  140.8 2.6 copy.60
  144.7 108.7 %while.13 = (s32[]{:T(128)}, f32[2,1,128,128]{3,2,0,1:T(8,128)S(1)}, f32[16,2,64,1,128]{4,2,0,1,3:T(8,128)}, s32[16]{0:T(128)S(1)}, s32[2]{0:T(128)S(1)}, /*inde...) while((s32[]{:T(128)}, ...), condition=%wide.region_2.3_spmd.clone, body=%wide.region_0.2_spmd.clone.sunk | while | flops 77050048 | bytes 1596940 | solution.py:96
  148.4 1.7 fusion.93
  150.1 1.3 fusion.91
  155.2 1.7 fusion.93
  156.9 1.3 fusion.91
  162.0 1.7 fusion.93
  168.8 1.7 fusion.93
  170.5 1.3 fusion.91
  175.6 1.7 fusion.93
  177.3 1.3 fusion.91
  182.4 1.7 fusion.93
  184.1 1.3 fusion.91
  189.2 1.7 fusion.93
  196.0 1.7 fusion.93
  197.7 1.3 fusion.91
  202.8 1.7 fusion.93
  204.5 1.3 fusion.91
  209.6 1.7 fusion.93
  211.3 1.3 fusion.91
  216.4 1.7 fusion.93
  223.2 1.7 fusion.93
  229.9 1.7 fusion.93
  236.7 1.7 fusion.93
  243.5 1.7 fusion.93
  250.3 1.7 fusion.93
  254.0 1.6 fusion.49
  255.7 5.7 convolution_convert_fusion.1
  261.4 11.5 %copy.71 = bf16[2052,2048]{0,1:T(8,128)(2,1)} copy(bf16[2052,2048]{1,0:T(8,128)(2,1)} %convolution_convert_fusion.1) | data formatting | bytes 16809984
  274.8 74.0 %reduce-scatter.7.cloned.1.call-done = bf16[128,2052]{1,0:T(8,128)(2,1)} async-done(((bf16[2048,2052]{1,0:T(8,128)(2,1)}), bf16[128,2052]{1,0:T(8,128)(2,1)}) %reduce-scatter.7.cloned.1.call-update) | async-done | bytes 525328
  348.8 1.4 copy.72
  353.3 103.5 %all-reduce.3.cloned.1.call-done = f32[32832]{0:T(1024)} async-done(((f32[32832]{0:T(1024)}), f32[32832]{0:T(1024)}) %all-reduce.3.cloned.1.call-update) | async-done | bytes 131344
  460.1 66.4 %all-gather.13.cloned.1.call-done = bf16[2048,704]{0,1:T(8,128)(2,1)} async-done(((bf16[256,704]{0,1:T(8,128)(2,1)}), bf16[2048,704]{0,1:T(8,128)(2,1)}) %all-gather.13.cloned.1.call-update) | async-done | bytes 2883600 | tf_op jit(solution)/shard_map/all_gather | solution.py:135
  526.5 60.9 %all-gather.11.cloned.1.call-done = bf16[2052,2048]{1,0:T(8,128)(2,1)} async-done(((bf16[2052,128]{1,0:T(8,128)(2,1)}), bf16[2052,2048]{1,0:T(8,128)(2,1)}) %all-gather.11.cloned.1.call-update) | async-done | bytes 8405008 | tf_op jit(solution)/shard_map/all_gather | solution.py:133
  587.5 12.6 %fusion.60 = f32[2052,704]{0,1:T(8,128)} fusion(bf16[2052,2048]{1,0:T(8,128)(2,1)} %all-gather.11.cloned.1.call-done, bf16[2048,704]{0,1:T(8,128)(2,1)} %all-gather.13.cloned.1.call-done), kind=kOutput, calls=%fused_computation.85 | convolution fusion | flops 5917114368 | bytes 17067008 | tf_op jit(solution)/shard_map/dot_general | solution.py:11
  600.1 41.6 %all-gather.15.cloned.1.call-done = bf16[352,2048]{1,0:T(8,128)(2,1)} async-done(((bf16[352,256]{1,0:T(8,128)(2,1)}), bf16[352,2048]{1,0:T(8,128)(2,1)}) %all-gather.15.cloned.1.call-update) | async-done | bytes 1441808 | tf_op jit(solution)/shard_map/all_gather | solution.py:141
  641.6 11.1 %convolution_convert_fusion = bf16[2052,2048]{1,0:T(8,128)(2,1)} fusion(bf16[352,2048]{1,0:T(8,128)(2,1)} %all-gather.15.cloned.1.call-done, f32[2052,704]{0,1:T(8,128)} %fusion.60), kind=kOutput, calls=%fused_computation.48 | convolution fusion | flops 2967093504 | bytes 15625216 | tf_op jit(solution)/shard_map/dot_general | solution.py:139
  652.7 11.5 %copy.73 = bf16[2052,2048]{0,1:T(8,128)(2,1)} copy(bf16[2052,2048]{1,0:T(8,128)(2,1)} %convolution_convert_fusion) | data formatting | bytes 16809984
  664.3 74.4 %reduce-scatter.9.cloned.1.call-done = bf16[128,2052]{1,0:T(8,128)(2,1)} async-done(((bf16[2048,2052]{1,0:T(8,128)(2,1)}), bf16[128,2052]{1,0:T(8,128)(2,1)}) %reduce-scatter.9.cloned.1.call-update) | async-done | bytes 525328
  738.7 1.3 copy.74
  (250 shorter events, 82.7 us)
Async XLA Ops:
  7.2 1.9 copy-start
  7.2 3.5 copy-start.12
  7.2 58.9 %all-gather.9.cloned.1.call-start = ((), (), s32[]{:S(2)}) async-start(), calls=%async_computation.3 | async-start | bytes 1769472 | tf_op jit(solution)/shard_map/all_gather | solution.py:71
  9.0 118.4 %all-gather.7.cloned.1.call-start = ((), (), s32[]{:S(2)}) async-start(), calls=%async_computation.2 | async-start | bytes 8947712 | tf_op jit(solution)/shard_map/all_gather | solution.py:68
  10.6 338.2 %reduce-scatter.7.cloned.1.call-start = ((), (), s32[]{:S(2)}) async-start(), calls=%async_computation.8 | async-start | bytes 9469952
  134.8 1.7 copy-start.3
  136.5 0.7 copy-start.15
  137.2 2.3 copy-start.4
  137.3 3.4 copy-start.1
  143.3 1.3 slice-start
  143.3 1.3 copy-start.16
  144.7 108.8 %copy-start.11 = (f32[4,1,128,128]{3,2,1,0:T(8,128)S(1)}, f32[4,1,128,128]{3,2,1,0:T(8,128)}, u32[]{:S(2)}) copy-start(f32[4,1,128,128]{3,2,1,0:T(8,128)} %param.16) | copy-start | bytes 786436
  253.4 8.0 %copy-start.5 = (f32[2,1,128,128]{3,2,0,1:T(8,128)}, f32[2,1,128,128]{3,2,0,1:T(8,128)S(1)}, u32[]{:S(2)}) copy-start(f32[2,1,128,128]{3,2,0,1:T(8,128)S(1)} %get-tuple-element.126) | copy-start | bytes 393220
  253.4 2.3 copy-start.2
  253.4 2.3 copy-start.6
  253.4 2.3 copy-start.14
  253.6 7.8 %copy-start.7 = (f32[4,1,128,128]{3,2,1,0:T(8,128)}, f32[4,1,128,128]{3,2,1,0:T(8,128)S(1)}, u32[]{:S(2)}) copy-start(f32[4,1,128,128]{3,2,1,0:T(8,128)S(1)} %multiply_add_fusion) | copy-start | bytes 786436
  272.9 0.7 copy-start.17
  272.9 77.3 %copy-start.13 = (bf16[4,128]{1,0:T(4,128)(2,1)S(1)}, bf16[4,128]{1,0:T(4,128)(2,1)}, u32[]{:S(2)}) copy-start(bf16[4,128]{1,0:T(4,128)(2,1)} %param.14) | copy-start | bytes 3076
  272.9 183.9 %all-reduce.3.cloned.1.call-start = ((), (), s32[]{:S(2)}) async-start(), calls=%async_computation.7 | async-start | bytes 270336
  348.8 2.9 copy-start.8
  351.0 0.6 copy-start.9
  351.6 174.9 %all-gather.13.cloned.1.call-start = ((), (), s32[]{:S(2)}) async-start(), calls=%async_computation.5 | async-start | bytes 3244032 | tf_op jit(solution)/shard_map/all_gather | solution.py:135
  352.5 235.0 %all-gather.11.cloned.1.call-start = ((), (), s32[]{:S(2)}) async-start(), calls=%async_computation.4 | async-start | bytes 8947712 | tf_op jit(solution)/shard_map/all_gather | solution.py:133
  457.9 1.3 copy-start.10
  459.1 182.5 %all-gather.15.cloned.1.call-start = ((), (), s32[]{:S(2)}) async-start(), calls=%async_computation.6 | async-start | bytes 1622016 | tf_op jit(solution)/shard_map/all_gather | solution.py:141
  459.9 278.8 %reduce-scatter.9.cloned.1.call-start = ((), (), s32[]{:S(2)}) async-start(), calls=%async_computation.9 | async-start | bytes 9469952
Sparse Core Ops, SparseCore 0:
  10.9 55.1 all-gather.8
  67.7 59.6 all-gather.6
  273.1 75.6 reduce-scatter.6
  351.7 105.0 all-reduce.2
  459.7 66.8 all-gather.12
  528.1 59.3 all-gather.10
  589.9 51.6 all-gather.14
  664.4 74.2 reduce-scatter.8
